TPU v7x, 256 devices: a whole 4x4x8 slice. The times are simulated.
256 devices in a mesh: acct: 64 (over z, x, core), rep: 4 (over y).
Axes of the slice: x: 4, y: 4, z: 8, core: 2. Of those that a mesh axis runs over, the one named last changes fastest.
Arguments:
- memory: bfloat16 [128, 512, 512], P('rep', 'acct'), may hold values from -3 to 3
- src_dev: int32 [3, 2048, 1], replicated, may hold values from 0 to 63; in each aligned block of 32 rows (0 to 31, 32 to 63, ..., all dimensions but the last counted through in order) at most 2 rows name the same one
- src_local: int32 [3, 2048], replicated, may hold values from 0 to 7
- dst_local: int32 [3, 2048], P(None, 'acct'), may hold values from 0 to 7
- delta_t: float32 [3, 2048], P(None, 'acct'), may hold values from 0.1 to 30
- masks: int32 [3, 2048, 128, 128], P(None, 'acct', 'rep'), may hold values 0 or 1
- member: int32 [3, 128, 512], P(None, 'rep', 'acct'), may hold values 0 or 1
- w_msg1: bfloat16 [512, 512], replicated, may hold values from -0.25 to 0.25
- b_msg1: float32 [512], replicated, may hold values from -3 to 3
- omega: float32 [512], replicated, may hold values from 0.05 to 3
- w_msg2: bfloat16 [512, 512], replicated, may hold values from -0.25 to 0.25
- ln_gain: float32 [512], replicated, may hold values from 0.25 to 1.75
- w_in: bfloat16 [512, 1536], replicated, may hold values from -0.25 to 0.25
- w_hid: bfloat16 [512, 1536], replicated, may hold values from -0.25 to 0.25
- b_in: float32 [1536], replicated, may hold values from -3 to 3
- b_hid: float32 [1536], replicated, may hold values from -3 to 3
Outputs:
- new_memory: bfloat16 [128, 512, 512], P('rep', 'acct')
Inputs may be any that keep to these rules, and one draw needn't show every extreme that they name: In each batch, among the 32 tiles of one index of acct (rows t of one aligned block), at most 2 have the same src_dev.
All inputs are finite; a program needn't handle non-finite values. No bound on the sum of `masks` or of `member` on one device may be relied on, other than what follows from the above.
Results may differ from a plain program's by a relative error of at most 0.009.
Values may be sent and summed in bfloat16 or wider, within the bound.
No kernel may reach another device: no remote copies, remote signals or barrier semaphores. Data moves between devices by JAX's collectives and lax.ppermute only.
A program may use at most 128 MiB of HBM per device.

v0:
```python
import jax
import jax.numpy as jnp
from jax import lax
from jax.sharding import PartitionSpec as P

NB = 3


def per_device(
    memory,
    src_dev,
    src_local,
    dst_local,
    delta_t,
    masks,
    member,
    w_msg1,
    b_msg1,
    omega,
    w_msg2,
    ln_gain,
    w_in,
    w_hid,
    b_in,
    b_hid,
):
    quarter, blk_dev, width = memory.shape
    peers = lax.axis_size("acct")
    myself = lax.axis_index("acct")
    til_dev = dst_local.shape[1]
    capacity = max(2, 2 * til_dev // peers)
    state = memory
    tile_ids = jnp.arange(til_dev, dtype=jnp.int32)
    earlier = (tile_ids[None, :] < tile_ids[:, None]).astype(jnp.int32)
    for batch in range(NB):
        sources = src_dev[batch, :, 0].reshape(peers, til_dev)
        locals_all = src_local[batch].reshape(peers, til_dev)
        mine = (sources == myself).astype(jnp.int32)
        ranks = jnp.cumsum(mine, axis=1) - mine
        my_sources = lax.dynamic_slice_in_dim(sources, myself, 1, 0)[0]
        same_source = (my_sources[:, None] == my_sources[None, :]).astype(jnp.int32)
        my_ranks = jnp.sum(same_source * earlier, axis=1)
        table = state
        slots = jnp.arange(capacity, dtype=jnp.int32)
        picker = mine[:, :, None] * (ranks[:, :, None] == slots[None, None, :]).astype(jnp.int32)
        send_index = jnp.sum(picker * locals_all[:, :, None], axis=1).reshape(-1)
        outgoing = jnp.take(table, send_index, axis=1)
        incoming = lax.all_to_all(outgoing, "acct", split_axis=1, concat_axis=1, tiled=True)
        rows = jnp.take(incoming, my_sources * capacity + my_ranks, axis=1)
        pre = jnp.einsum("stc,ch->sth", rows, w_msg1, preferred_element_type=jnp.float32).astype(
            jnp.bfloat16
        )
        code = jnp.cos(delta_t[batch][:, None] * omega[None, :])
        hidden = jax.nn.relu(pre.astype(jnp.float32) + b_msg1 + code[None]).astype(jnp.bfloat16)
        message = jnp.einsum(
            "sth,hd->std", hidden, w_msg2, preferred_element_type=jnp.float32
        ).astype(jnp.bfloat16)
        tile_bits = masks[batch].astype(jnp.bfloat16)
        onehot = (
            dst_local[batch][:, None] == jnp.arange(blk_dev, dtype=jnp.int32)[None, :]
        ).astype(jnp.float32)
        partial_value = jnp.einsum(
            "tsd,ste->dte", tile_bits, message, preferred_element_type=jnp.float32
        )
        agg = lax.psum_scatter(
            jnp.einsum("dte,tb->dbe", partial_value, onehot), "rep", scatter_dimension=0, tiled=True
        )
        mean = jnp.mean(agg, axis=-1, keepdims=True)
        var = jnp.mean((agg - mean) ** 2, axis=-1, keepdims=True)
        normed = ((agg - mean) * lax.rsqrt(var + 1e-05) * ln_gain).astype(jnp.bfloat16)
        gin = jnp.einsum("sbd,dk->sbk", normed, w_in, preferred_element_type=jnp.float32) + b_in
        ghid = jnp.einsum("sbd,dk->sbk", state, w_hid, preferred_element_type=jnp.float32) + b_hid
        zgate = jax.nn.sigmoid(gin[..., :width] + ghid[..., :width])
        rgate = jax.nn.sigmoid(gin[..., width : 2 * width] + ghid[..., width : 2 * width])
        cand = jnp.tanh(gin[..., 2 * width :] + rgate * ghid[..., 2 * width :])
        fresh = (1.0 - zgate) * cand + zgate * state.astype(jnp.float32)
        state = jnp.where(member[batch][:, :, None] == 1, fresh.astype(jnp.bfloat16), state)
    return state


def solution(mesh):
    placed = (
        P("rep", "acct", None),
        P(),
        P(),
        P(None, "acct"),
        P(None, "acct"),
        P(None, "acct", "rep", None),
        P(None, "rep", "acct"),
        P(),
        P(),
        P(),
        P(),
        P(),
        P(),
        P(),
        P(),
        P(),
    )
    return jax.shard_map(
        per_device, mesh=mesh, in_specs=placed, out_specs=P("rep", "acct", None), check_vma=False
    )
```

profile of v0, /device:TPU:1, one launch (start us, length us, event | category | flops | bytes accessed | tf_op | source)
XLA Modules:
  0.0 564.2 jit_solution(3315488211553951467)
XLA Ops:
  10.5 24.7 %gather_fusion = bf16[128,32,512]{2,0,1:T(8,128)(2,1)} fusion(bf16[32,8,512]{2,1,0:T(8,128)(2,1)S(1)} %copy-done.1, s32[1024]{0:T(1024)S(1)} %pad_clamp_fusion.5), kind=kCustom, calls=%fused_computation.clone | custom fusion | bytes 8389120 | tf_op jit(solution)/shard_map/jit(_take)/gather | solution.py:47
  35.2 2.6 select_bitcast_fusion.2
  37.8 4.4 copy.56
  42.2 13.3 %all-to-all-start = ((bf16[32,128,512]{2,0,1:T(8,128)(2,1)}), bf16[32,128,512]{2,0,1:T(8,128)(2,1)}, u32[]{:S(2)}, u32[]{:S(2)}) async-start(bf16[32,128,512]{2,0,1:T(8,128)(2,1)} %copy.56), calls=%async_computation | async-start | bytes 8388608 | tf_op jit(solution)/shard_map/all_to_all | solution.py:48
  60.2 89.7 %all-to-all-done = bf16[32,128,512]{2,0,1:T(8,128)(2,1)} async-done(((bf16[32,128,512]{2,0,1:T(8,128)(2,1)}), bf16[32,128,512]{2,0,1:T(8,128)(2,1)}, u32[]{:S(2)}, u32[]{:S(2)}) %all-to-all-start) | async-done | bytes 4194336 | tf_op jit(solution)/shard_map/all_to_all | solution.py:48
  149.9 2.8 gather_fusion.1
  153.9 3.0 convolution_convert_fusion.4
  156.9 4.5 convolution_bitcast_fusion.2
  161.4 8.0 %copy.59 = bf16[128,32,512]{2,1,0:T(8,128)(2,1)} copy(bf16[128,32,512]{0,2,1:T(8,128)(2,1)} %convolution_bitcast_fusion.2) | data formatting | bytes 8388608 | tf_op jit(solution)/shard_map/tsd,ste->dte/transpose | solution.py:62
  169.4 4.2 convolution_bitcast_fusion.5
  179.7 24.3 %reduce-scatter.4.cloned.1.call-done = f32[32,8,512]{2,1,0:T(8,128)} async-done(((f32[128,8,512]{2,1,0:T(8,128)}), f32[32,8,512]{2,1,0:T(8,128)}) %reduce-scatter.4.cloned.1.call-update) | async-done | bytes 524304 | tf_op jit(solution)/shard_map/reduce_scatter | solution.py:65
  209.5 2.8 gather_fusion.2
  212.3 4.6 select_bitcast_fusion.1
  216.9 10.9 %all-to-all-start.1 = ((bf16[32,128,512]{2,0,1:T(8,128)(2,1)}), bf16[32,128,512]{2,0,1:T(8,128)(2,1)}, u32[]{:S(2)}, u32[]{:S(2)}) async-start(bf16[32,128,512]{2,0,1:T(8,128)(2,1)} %select_bitcast_fusion.1), calls=%async_computation.2 | async-start | bytes 8388608 | tf_op jit(solution)/shard_map/all_to_all | solution.py:48
  228.3 93.9 %all-to-all-done.1 = bf16[32,128,512]{2,0,1:T(8,128)(2,1)} async-done(((bf16[32,128,512]{2,0,1:T(8,128)(2,1)}), bf16[32,128,512]{2,0,1:T(8,128)(2,1)}, u32[]{:S(2)}, u32[]{:S(2)}) %all-to-all-start.1) | async-done | bytes 4194336 | tf_op jit(solution)/shard_map/all_to_all | solution.py:48
  322.2 3.8 gather_fusion.3
  328.4 4.0 convolution_convert_fusion.2
  332.3 4.8 convolution_bitcast_fusion.1
  337.1 8.0 %copy.63 = bf16[128,32,512]{2,1,0:T(8,128)(2,1)} copy(bf16[128,32,512]{0,2,1:T(8,128)(2,1)} %convolution_bitcast_fusion.1) | data formatting | bytes 8388608 | tf_op jit(solution)/shard_map/tsd,ste->dte/transpose | solution.py:62
  345.1 4.2 convolution_bitcast_fusion.4
  352.0 26.0 %reduce-scatter.6.cloned.1.call-done = f32[32,8,512]{2,1,0:T(8,128)} async-done(((f32[128,8,512]{2,1,0:T(8,128)}), f32[32,8,512]{2,1,0:T(8,128)}) %reduce-scatter.6.cloned.1.call-update) | async-done | bytes 524304 | tf_op jit(solution)/shard_map/reduce_scatter | solution.py:65
  383.5 2.8 gather_fusion.4
  386.2 4.6 select_bitcast_fusion
  390.9 10.8 %all-to-all-start.2 = ((bf16[32,128,512]{2,0,1:T(8,128)(2,1)}), bf16[32,128,512]{2,0,1:T(8,128)(2,1)}, u32[]{:S(2)}, u32[]{:S(2)}) async-start(bf16[32,128,512]{2,0,1:T(8,128)(2,1)} %select_bitcast_fusion), calls=%async_computation.4 | async-start | bytes 8388608 | tf_op jit(solution)/shard_map/all_to_all | solution.py:48
  402.2 93.9 %all-to-all-done.2 = bf16[32,128,512]{2,0,1:T(8,128)(2,1)} async-done(((bf16[32,128,512]{2,0,1:T(8,128)(2,1)}), bf16[32,128,512]{2,0,1:T(8,128)(2,1)}, u32[]{:S(2)}, u32[]{:S(2)}) %all-to-all-start.2) | async-done | bytes 4194336 | tf_op jit(solution)/shard_map/all_to_all | solution.py:48
  496.1 3.8 gather_fusion.5
  499.9 2.4 select_bitcast_fusion.3
  502.3 4.0 convolution_convert_fusion
  506.3 4.8 convolution_bitcast_fusion
  511.0 7.9 %copy.67 = bf16[128,32,512]{2,1,0:T(8,128)(2,1)} copy(bf16[128,32,512]{0,2,1:T(8,128)(2,1)} %convolution_bitcast_fusion) | data formatting | bytes 8388608 | tf_op jit(solution)/shard_map/tsd,ste->dte/transpose | solution.py:62
  519.0 4.2 convolution_bitcast_fusion.3
  525.9 26.0 %reduce-scatter.8.cloned.1.call-done = f32[32,8,512]{2,1,0:T(8,128)} async-done(((f32[128,8,512]{2,1,0:T(8,128)}), f32[32,8,512]{2,1,0:T(8,128)}) %reduce-scatter.8.cloned.1.call-update) | async-done | bytes 524304 | tf_op jit(solution)/shard_map/reduce_scatter | solution.py:65
  (157 shorter events, 40.4 us)
Async XLA Ops:
  6.5 171.4 %copy-start = (bf16[512,1536]{1,0:T(8,128)(2,1)S(1)}, bf16[512,1536]{1,0:T(8,128)(2,1)}, u32[]{:S(2)}) copy-start(bf16[512,1536]{1,0:T(8,128)(2,1)} %param.33) | copy-start | bytes 4718596
  6.5 3.9 copy-start.1
  42.2 13.5 %copy-start.10 = (s32[3,32,32,128]{3,2,1,0:T(8,128)S(1)}, s32[3,32,32,128]{3,2,1,0:T(8,128)}, u32[]{:S(2)}) copy-start(s32[3,32,32,128]{3,2,1,0:T(8,128)} %param.25) | copy-start | bytes 4718596
  42.2 107.7 %all-to-all-start = ((bf16[32,128,512]{2,0,1:T(8,128)(2,1)}), bf16[32,128,512]{2,0,1:T(8,128)(2,1)}, u32[]{:S(2)}, u32[]{:S(2)}) async-start(bf16[32,128,512]{2,0,1:T(8,128)(2,1)} %copy.56), calls=%async_computation | async-start | bytes 8388608 | tf_op jit(solution)/shard_map/all_to_all | solution.py:48
  55.5 2.0 copy-start.27
  55.5 2.1 copy-start.28
  55.6 148.5 %reduce-scatter.4.cloned.1.call-start = ((), (), s32[]{:S(2)}) async-start(), calls=%async_computation.6 | async-start | bytes 2621440 | tf_op jit(solution)/shard_map/reduce_scatter | solution.py:65
  60.2 93.7 %copy-start.29 = (f32[512]{0:T(512)S(1)}, f32[512]{0:T(512)}, u32[]{:S(2)}) copy-start(f32[512]{0:T(512)} %param.28) | copy-start | bytes 6148
  173.5 1.0 copy-start.18
  173.5 2.3 copy-start.14
  173.6 4.4 copy-start.11
  177.9 28.7 %copy-start.2 = (bf16[512,1536]{1,0:T(8,128)(2,1)S(1)}, bf16[512,1536]{1,0:T(8,128)(2,1)}, u32[]{:S(2)}) copy-start(bf16[512,1536]{1,0:T(8,128)(2,1)} %param.32) | copy-start | bytes 4718596
  177.9 28.7 %copy-start.12 = (f32[1536]{0:T(1024)S(1)}, f32[1536]{0:T(1024)}, u32[]{:S(2)}) copy-start(f32[1536]{0:T(1024)} %param.34) | copy-start | bytes 18436
  177.9 28.7 %copy-start.16 = (f32[512]{0:T(512)S(1)}, f32[512]{0:T(512)}, u32[]{:S(2)}) copy-start(f32[512]{0:T(512)} %param.31) | copy-start | bytes 6148
  205.2 3.1 copy-start.5
  205.2 3.1 copy-start.17
  208.7 0.7 copy-start.8
  209.5 2.8 copy-start.25
  216.9 11.2 %copy-start.26 = (s32[32]{0:T(128)S(1)}, s32[32]{0:T(128)}, u32[]{:S(2)}) copy-start(s32[32]{0:T(128)} %get-tuple-element.34) | copy-start | bytes 388
  216.9 105.3 %all-to-all-start.1 = ((bf16[32,128,512]{2,0,1:T(8,128)(2,1)}), bf16[32,128,512]{2,0,1:T(8,128)(2,1)}, u32[]{:S(2)}, u32[]{:S(2)}) async-start(bf16[32,128,512]{2,0,1:T(8,128)(2,1)} %select_bitcast_fusion.1), calls=%async_computation.2 | async-start | bytes 8388608 | tf_op jit(solution)/shard_map/all_to_all | solution.py:48
  227.8 150.2 %reduce-scatter.6.cloned.1.call-start = ((), (), s32[]{:S(2)}) async-start(), calls=%async_computation.7 | async-start | bytes 2621440 | tf_op jit(solution)/shard_map/reduce_scatter | solution.py:65
  228.3 100.1 %copy-start.13 = (f32[32,512]{1,0:T(8,128)S(1)}, f32[32,512]{1,0:T(8,128)}, u32[]{:S(2)}) copy-start(f32[32,512]{1,0:T(8,128)} %get-tuple-element.26) | copy-start | bytes 196612
  228.3 100.1 %copy-start.30 = (f32[512]{0:T(512)S(1)}, f32[512]{0:T(512)}, u32[]{:S(2)}) copy-start(f32[512]{0:T(512)} %param.28) | copy-start | bytes 6148
  337.1 8.0 %copy-start.22 = (s32[32]{0:T(128)S(1)}, s32[32]{0:T(128)}, u32[]{:S(2)}) copy-start(s32[32]{0:T(128)} %get-tuple-element.24) | copy-start | bytes 388
  349.3 1.0 copy-start.9
  379.2 3.1 copy-start.4
  390.9 105.2 %all-to-all-start.2 = ((bf16[32,128,512]{2,0,1:T(8,128)(2,1)}), bf16[32,128,512]{2,0,1:T(8,128)(2,1)}, u32[]{:S(2)}, u32[]{:S(2)}) async-start(bf16[32,128,512]{2,0,1:T(8,128)(2,1)} %select_bitcast_fusion), calls=%async_computation.4 | async-start | bytes 8388608 | tf_op jit(solution)/shard_map/all_to_all | solution.py:48
  401.7 150.2 %reduce-scatter.8.cloned.1.call-start = ((), (), s32[]{:S(2)}) async-start(), calls=%async_computation.8 | async-start | bytes 2621440 | tf_op jit(solution)/shard_map/reduce_scatter | solution.py:65
  402.2 100.1 %copy-start.31 = (f32[512]{0:T(512)S(1)}, f32[512]{0:T(512)}, u32[]{:S(2)}) copy-start(f32[512]{0:T(512)} %param.28) | copy-start | bytes 6148
  511.0 7.9 %copy-start.21 = (s32[32]{0:T(128)S(1)}, s32[32]{0:T(128)}, u32[]{:S(2)}) copy-start(s32[32]{0:T(128)} %get-tuple-element.22) | copy-start | bytes 388
  523.2 1.0 copy-start.7
  553.0 3.1 copy-start.3
  (6 other events, 3.8 us)
Sparse Core Ops, SparseCore 0:
  173.7 30.2 reduce-scatter.3
  349.5 28.5 reduce-scatter.5
  523.3 28.4 reduce-scatter.7
where the time goes:
time: 570 us; the launch traced here: 564 us
  waiting for transfers between devices  354 us (62%)
  local copies, waits for them, and re-layouts  80 us (14%)
  matrix products  47.8 us (8%)
  starting transfers between devices  35.6 us (6%)
  other arithmetic  32.7 us (6%)
  between operations  14.1 us (2%)
    all_to_all x3, waiting for transfers between devices, per_device(): lax.all_to_all(outgoing, 'acct', split_axis=1, concat_axis=1, tiled=True)  278 us
    reduce_scatter x3, waiting for transfers between devices, per_device(): lax.psum_scatter(jnp.einsum('dte,tb->dbe', partial_value, onehot), 'rep',...  76.4 us
    all_to_all x3, starting transfers between devices, per_device(): lax.all_to_all(outgoing, 'acct', split_axis=1, concat_axis=1, tiled=True)  35 us
    gather x3, local copies, waits for them, and re-layouts, per_device(): outgoing = jnp.take(table, send_index, axis=1)  30.3 us
    transpose x3, local copies, waits for them, and re-layouts, per_device(): jnp.einsum('tsd,ste->dte', tile_bits, message, preferred_element_type=jnp...  23.9 us
    dot_general x3, matrix products, per_device(): jnp.einsum('tsd,ste->dte', tile_bits, message, preferred_element_type=jnp...  14.1 us
    dot_general x3, matrix products, per_device(): jnp.einsum('dte,tb->dbe', partial_value, onehot)  12.6 us
    select_n x6, other arithmetic, per_device(): outgoing = jnp.take(table, send_index, axis=1)  11.8 us
  transfers between devices with their start and end apart: 6, of which 6 were waited for; matrix products, arithmetic and copies ran while one was open for 2% of the time, Pallas kernels for 0%

commit v1 on v0

v1 whole, which is shorter than its diff:
```python
import functools

import jax
import jax.numpy as jnp
from jax import lax
from jax.experimental import pallas as pl
from jax.experimental.pallas import tpu as pltpu
from jax.sharding import PartitionSpec as P

NB = 3
NZ, NX, NC, NR = 8, 4, 2, 4
BD, TD, ROWS, D = 8, 32, 32, 512
CAP = 32
COL = NZ * BD
BF, F32 = jnp.bfloat16, jnp.float32

ANY = pl.BlockSpec(memory_space=pl.ANY)
SMEM = pl.BlockSpec(memory_space=pltpu.SMEM)
VMEM = pl.BlockSpec(memory_space=pltpu.VMEM)


def z_shift(s):
    n = NX * NC
    return [(i, ((i // n + s) % NZ) * n + i % n) for i in range(NZ * n)]


def x_shift(s):
    n = NX * NC
    return [(i, (i // n) * n + ((i // NC + s) % NX) * NC + i % NC) for i in range(NZ * n)]


def core_swap():
    return [(i, i ^ 1) for i in range(NZ * NX * NC)]


def rep_shift(s):
    return [(i, (i + s) % NR) for i in range(NR)]


def start_from(table, place, dst, sem):
    low = 0
    for ref in table:
        high = low + ref.shape[0]

        @pl.when((place >= low) & (place < high))
        def _(ref=ref, low=low):
            pltpu.make_async_copy(ref.at[place - low], dst, sem).start()

        low = high


def pick_kernel(counts, idx_ref, *refs):
    n_out = len(counts)
    sem = refs[-1]
    table = refs[: len(refs) - 1 - n_out]
    outs = refs[len(refs) - 1 - n_out : -1]
    base = 0
    for o, (out, count) in enumerate(zip(outs, counts)):

        def body(s, carry, out=out, base=base, o=o):
            start_from(table, idx_ref[base + s], out.at[s], sem.at[o])
            return carry

        lax.fori_loop(0, count, body, 0)
        base += count
    for o, out in enumerate(outs):
        pltpu.make_async_copy(out, out, sem.at[o]).wait()


def pick(idx, table, counts):
    return pl.pallas_call(
        functools.partial(pick_kernel, counts),
        out_shape=[jax.ShapeDtypeStruct((n, ROWS, D), BF) for n in counts],
        in_specs=[SMEM] + [ANY] * len(table),
        out_specs=[ANY] * len(counts),
        scratch_shapes=[pltpu.SemaphoreType.DMA((len(counts),))],
        name="pick",
    )(idx, *table)


def message_kernel(n_table, rep_ref, idx_ref, code_ref, w2_ref, mask_ref, hot_ref, *refs):
    table = refs[:n_table]
    own_ref, out1, out2, out3, rows_ref, lhs_ref, sem = refs[n_table:]

    def body(t, carry):
        start_from(table, idx_ref[t], rows_ref.at[t], sem)
        return carry

    lax.fori_loop(0, TD, body, 0)
    rep = rep_ref[0]
    for j in range(NR):
        r = lax.rem(rep + j, NR)
        quarter = mask_ref[pl.ds(pl.multiple_of(r * ROWS, ROWS), ROWS), :]
        for k in range(BD):
            lhs_ref[pl.ds((j * BD + k) * ROWS, ROWS), :] = quarter * hot_ref[k : k + 1, :]
    pltpu.make_async_copy(rows_ref, rows_ref, sem).wait()
    hidden = rows_ref[...].astype(F32) + code_ref[...][:, None, :]
    hidden = jnp.maximum(hidden, 0.0).astype(BF).reshape(TD * ROWS, D)
    message = jnp.dot(hidden, w2_ref[...], preferred_element_type=F32).astype(BF)
    agg = jnp.dot(lhs_ref[...], message, preferred_element_type=F32)
    n = BD * ROWS
    own_ref[...] = agg[:n]
    out1[...] = agg[n : 2 * n].astype(BF)
    out2[...] = agg[2 * n : 3 * n].astype(BF)
    out3[...] = agg[3 * n :].astype(BF)


def message_call(rep, idx, code, w2, mask, hot, table):
    n = BD * ROWS
    return pl.pallas_call(
        functools.partial(message_kernel, len(table)),
        out_shape=[jax.ShapeDtypeStruct((n, D), F32)] + [jax.ShapeDtypeStruct((n, D), BF)] * 3,
        in_specs=[SMEM, SMEM, VMEM, VMEM, VMEM, VMEM] + [ANY] * len(table),
        out_specs=[VMEM] * 4,
        scratch_shapes=[
            pltpu.VMEM((TD, ROWS, D), BF),
            pltpu.VMEM((NR * n, TD * ROWS), BF),
            pltpu.SemaphoreType.DMA(()),
        ],
        compiler_params=pltpu.CompilerParams(vmem_limit_bytes=32 << 20),
        name="message",
    )(rep, idx, code, w2, mask, hot, *table)


def sigmoid(v):
    return 0.5 * jnp.tanh(0.5 * v) + 0.5


def update_kernel(last, own, in1, in2, in3, state, member, gain, w_in, w_hid, b_in, b_hid, w1, *outs):
    total = own[...] + in1[...].astype(F32) + in2[...].astype(F32) + in3[...].astype(F32)
    mean = jnp.mean(total, axis=-1, keepdims=True)
    centred = total - mean
    var = jnp.mean(centred * centred, axis=-1, keepdims=True)
    x = (centred * lax.rsqrt(var + 1e-05) * gain[...]).astype(BF)
    old = state[...]
    gin = jnp.dot(x, w_in[...], preferred_element_type=F32) + b_in[...]
    ghid = jnp.dot(old, w_hid[...], preferred_element_type=F32) + b_hid[...]
    z = sigmoid(gin[:, :D] + ghid[:, :D])
    r = sigmoid(gin[:, D : 2 * D] + ghid[:, D : 2 * D])
    cand = jnp.tanh(gin[:, 2 * D :] + r * ghid[:, 2 * D :])
    fresh = (1.0 - z) * cand + z * old.astype(F32)
    new = jnp.where(member[...] == 1, fresh, old.astype(F32)).astype(BF)
    outs[0][...] = new
    if not last:
        outs[1][...] = jnp.dot(new, w1[...], preferred_element_type=F32).astype(BF)


def update_call(last, *args):
    n = BD * ROWS
    outs = [jax.ShapeDtypeStruct((n, D), BF)] * (1 if last else 2)
    return pl.pallas_call(
        functools.partial(update_kernel, last),
        out_shape=outs,
        in_specs=[VMEM] * len(args),
        out_specs=[VMEM] * len(outs),
        compiler_params=pltpu.CompilerParams(vmem_limit_bytes=32 << 20),
        name="update",
    )(*args)


def first_kernel(state, w1, pre):
    pre[...] = jnp.dot(state[...], w1[...], preferred_element_type=F32).astype(BF)


def first_call(state, w1):
    return pl.pallas_call(
        first_kernel,
        out_shape=jax.ShapeDtypeStruct(state.shape, BF),
        in_specs=[VMEM] * 2,
        out_specs=VMEM,
        name="first",
    )(state, w1)


def places(src_dev, src_local):
    me = lax.axis_index("acct")
    z, x, c = me // (NX * NC), (me // NC) % NX, me % NC
    dev = src_dev.reshape(NB, NZ, NX, NC * TD)
    loc = src_local.reshape(NB, NZ, NX, NC * TD)
    dev = lax.dynamic_slice_in_dim(dev, z, 1, 1)[:, 0]
    loc = lax.dynamic_slice_in_dim(loc, z, 1, 1)[:, 0]
    sz, sx, sc = dev // (NX * NC), (dev // NC) % NX, dev % NC
    column = ((sz - z) % NZ) * BD + loc
    pair = sx * NC + sc
    tile = jnp.arange(NC * TD, dtype=jnp.int32)
    before = (tile[None, :] < tile[:, None]).astype(jnp.int32)
    rank = jnp.sum((pair[..., :, None] == pair[..., None, :]) * before, axis=-1)
    mine = pair == x * NC + c
    slots = jnp.arange(CAP, dtype=jnp.int32)
    chosen = mine[:, :, None, :] & (rank[:, :, None, :] == slots[None, None, :, None])
    out = jnp.sum(jnp.where(chosen, column[:, :, None, :], 0), axis=-1)
    lanes = (x + jnp.arange(1, NX, dtype=jnp.int32)) % NX
    turn = (lanes[:, None] == jnp.arange(NX, dtype=jnp.int32)[None, :]).astype(jnp.int32)
    send = jnp.sum(out[:, None, :, :] * turn[None, :, :, None], axis=2).reshape(NB, -1)
    here = (jnp.arange(NX, dtype=jnp.int32) == x).astype(jnp.int32)[None, :, None]
    column, rank, sx, sc = (jnp.sum(a * here, axis=1) for a in (column, rank, sx, sc))
    lane = (sx - x) % NX
    place = jnp.where(lane == 0, column, COL + (lane - 1) * CAP + rank)
    place = place.reshape(NB, NC, TD)
    local = (sc == c).reshape(NB, NC, TD)
    self_ = (jnp.arange(NC, dtype=jnp.int32) == c).astype(jnp.int32)[None, :, None]
    swapped = COL + (NX - 1) * CAP + jnp.arange(TD, dtype=jnp.int32)
    final = jnp.sum(jnp.where(local, place, swapped[None, None]) * self_, axis=1)
    swap = jnp.sum(jnp.where(local, place, 0) * (1 - self_), axis=1)
    return send, swap, final


def exchange(pre, send, swap):
    up, down = [pre], [pre]
    for step in range(3):
        up.append(lax.ppermute(up[-1], "acct", z_shift(1)))
        down.append(lax.ppermute(down[-1], "acct", z_shift(-1)))
    half = BD // 2
    far_up = lax.ppermute(up[3][:half], "acct", z_shift(1))
    far_down = lax.ppermute(down[3][half:], "acct", z_shift(-1))
    column = [pre, down[1], down[2], down[3], far_up, far_down, up[3], up[2], up[1]]
    outgoing = pick(send, column, (CAP,) * (NX - 1))
    arrived = [lax.ppermute(outgoing[d - 1], "acct", x_shift(d)) for d in range(1, NX)]
    table = column + arrived[::-1]
    [crossing] = pick(swap, table, (TD,))
    return table + [lax.ppermute(crossing, "acct", core_swap())]


def per_device(
    memory, src_dev, src_local, dst_local, delta_t, masks, member,
    w_msg1, b_msg1, omega, w_msg2, ln_gain, w_in, w_hid, b_in, b_hid,
):
    n = BD * ROWS
    rep = lax.axis_index("rep").reshape(1).astype(jnp.int32)
    state = jnp.swapaxes(memory, 0, 1).reshape(n, D)
    pre = first_call(state, w_msg1)
    send, swap, final = places(src_dev, src_local)
    code = jnp.cos(delta_t[:, :, None] * omega) + b_msg1
    mask = jnp.transpose(masks, (0, 3, 1, 2)).reshape(NB, NR * ROWS, TD * ROWS).astype(BF)
    hot = dst_local[:, None, :] == jnp.arange(BD, dtype=jnp.int32)[None, :, None]
    hot = jnp.repeat(hot.astype(BF), ROWS, axis=2)
    chosen = jnp.swapaxes(member, 1, 2).reshape(NB, n, 1)
    for batch in range(NB):
        table = exchange(pre.reshape(BD, ROWS, D), send[batch], swap[batch])
        own, *shares = message_call(
            rep, final[batch], code[batch], w_msg2, mask[batch], hot[batch], table
        )
        shares = [lax.ppermute(s, "rep", rep_shift(j + 1)) for j, s in enumerate(shares)]
        last = batch == NB - 1
        state, *rest = update_call(
            last, own, *shares, state, chosen[batch], ln_gain[None], w_in, w_hid, b_in[None], b_hid[None], w_msg1
        )
        if not last:
            pre = rest[0]
    return jnp.swapaxes(state.reshape(BD, ROWS, D), 0, 1)


def solution(mesh):
    placed = (
        P("rep", "acct", None),
        P(),
        P(),
        P(None, "acct"),
        P(None, "acct"),
        P(None, "acct", "rep", None),
        P(None, "rep", "acct"),
    ) + (P(),) * 9
    return jax.shard_map(
        per_device, mesh=mesh, in_specs=placed, out_specs=P("rep", "acct", None), check_vma=False
    )
```

time: 570 us -> 795 us (1.39)
  Pallas kernels: 0 us -> 421 us
  waiting for transfers between devices: 354 us -> 211 us
  matrix products: 47.8 us -> 0 us
  starting transfers between devices: 35.6 us -> 64.2 us
  other arithmetic: 32.7 us -> 4.26 us
  between operations: 14.1 us -> 1.01 us
    pallas_call x0 -> x13, Pallas kernels: none -> 421 us  [the longest x6 392 us: pick(): pl.pallas_call(functools.partial(pick_kernel, counts), out_shape=[jax.Sha...]
    all_to_all x3 -> x0, waiting for transfers between devices: 278 us -> none  [per_device(): lax.all_to_all(outgoing, 'acct', split_axis=1, concat_axis=1, tiled=True)]
    ppermute x0 -> x45, waiting for transfers between devices: none -> 211 us  [the longest x9 134 us: exchange(): lax.ppermute(outgoing[d - 1], 'acct', x_shift(d))]
    reduce_scatter x3 -> x0, waiting for transfers between devices: 76.4 us -> none  [per_device(): lax.psum_scatter(jnp.einsum('dte,tb->dbe', partial_value, onehot), 'rep',...]
    ppermute x0 -> x45, starting transfers between devices: none -> 64.2 us  [the longest x9 24.9 us: exchange(): down.append(lax.ppermute(down[-1], 'acct', z_shift(-1)))]
    unnamed x64 -> x186, local copies, waits for them, and re-layouts: 4.03 us -> 54.4 us
    dot_general x15 -> x0, matrix products: 47.8 us -> none  [the longest x3 14.1 us: per_device(): jnp.einsum('tsd,ste->dte', tile_bits, message, preferred_element_type=jnp...]
    gather x6 -> x0, local copies, waits for them, and re-layouts: 40.7 us -> none  [the longest x3 30.3 us: per_device(): outgoing = jnp.take(table, send_index, axis=1)]
  transfers between devices with their start and end apart: 6 -> 45, of which waited for: 6 -> 26; matrix products, arithmetic and copies ran while one was open for 2% -> 4% of each run, Pallas kernels for 0% -> 0%
where the time goes in v1:
time: 795 us; the launch traced here: 785 us
  Pallas kernels  421 us (53%)
  waiting for transfers between devices  211 us (27%)
  local copies, waits for them, and re-layouts  83.5 us (11%)
  starting transfers between devices  64.2 us (8%)
    pallas_call x6, Pallas kernels, pick(): pl.pallas_call(functools.partial(pick_kernel, counts), out_shape=[jax.Sha...  392 us
    ppermute x9, waiting for transfers between devices, exchange(): lax.ppermute(outgoing[d - 1], 'acct', x_shift(d))  134 us
    unnamed x186, local copies, waits for them, and re-layouts  54.4 us
    ppermute x9, waiting for transfers between devices, exchange(): up.append(lax.ppermute(up[-1], 'acct', z_shift(1)))  40.7 us
    ppermute x9, waiting for transfers between devices, per_device(): lax.ppermute(s, 'rep', rep_shift(j + 1))  32.4 us
    ppermute x9, starting transfers between devices, exchange(): down.append(lax.ppermute(down[-1], 'acct', z_shift(-1)))  24.9 us
    pallas_call x3, Pallas kernels, message_call(): pl.pallas_call(functools.partial(message_kernel, len(table)), out_shape=[...  19.4 us
  transfers between devices with their start and end apart: 45, of which 26 were waited for; matrix products, arithmetic and copies ran while one was open for 4% of the time, Pallas kernels for 0%

profile of v1, /device:TPU:1, one launch (start us, length us, event | category | flops | bytes accessed | tf_op | source)
XLA Modules:
  0.0 785.3 jit_solution(1185556949739145448)
XLA Ops:
  6.5 3.9 collective-permute-start
  11.7 4.9 collective-permute-done.3.refs_8_
  20.6 3.8 collective-permute-done.4.refs_7_
  37.7 97.1 %pick.6 = (bf16[32,32,512]{2,1,0:T(8,128)(2,1)}, bf16[32,32,512]{2,1,0:T(8,128)(2,1)}, bf16[32,32,512]{2,1,0:T(8,128)(2,1)}) custom-call(s32[96]{0:T(128)} %squeeze.74.idx_ref, bf16[8,32,512]{2,1,0:T(8,128)(2,1)} %bitcast.71, bf16[8,32,512]{2,1,0:T(8,128)(2,1)} %copy-done.30, bf16[8,32,512]{2,1,0:T(8,128)(2,1)} %copy-done.34, ...), custom_call_target="tpu_custom_call" | custom-call | tf_op jit(solution)/shard_map/pick/pallas_call | solution.py:71
  143.3 13.5 %collective-permute-done.10.refs_11_ = bf16[32,32,512]{2,1,0:T(8,128)(2,1)S(1)} collective-permute-done((bf16[32,32,512]{2,1,0:T(8,128)(2,1)}, bf16[32,32,512]{2,1,0:T(8,128)(2,1)S(1)}, u32[]{:S(2)}, u32[]{:S(2)}) %collective-permute-start.10) | collective-permute-done | bytes 1048608 | tf_op jit(solution)/shard_map/ppermute | solution.py:218
  156.8 23.4 %collective-permute-done.9.refs_10_ = bf16[32,32,512]{2,1,0:T(8,128)(2,1)S(1)} collective-permute-done((bf16[32,32,512]{2,1,0:T(8,128)(2,1)}, bf16[32,32,512]{2,1,0:T(8,128)(2,1)S(1)}, u32[]{:S(2)}, u32[]{:S(2)}) %collective-permute-start.9) | collective-permute-done | bytes 1048608 | tf_op jit(solution)/shard_map/ppermute | solution.py:218
  181.2 33.7 %pick.7 = bf16[32,32,512]{2,1,0:T(8,128)(2,1)} custom-call(s32[32]{0:T(128)} %get-tuple-element.84.idx_ref, bf16[8,32,512]{2,1,0:T(8,128)(2,1)} %bitcast.72, bf16[8,32,512]{2,1,0:T(8,128)(2,1)} %copy-done.30, bf16[8,32,512]{2,1,0:T(8,128)(2,1)} %copy-done.34, bf16[8,32,512]{2,1,0:T(8,128)(2,1)} %copy-done.17, bf16[4,32,512]{2,1,0:T(8,128)(2,1)} %copy-done.56, ...), custom_call_target="tpu_custom_call" | custom-call | tf_op jit(solution)/shard_map/pick/pallas_call | solution.py:71
  214.9 5.4 collective-permute-start.11
  239.0 7.2 message.3
  256.5 6.9 collective-permute-done.13.in2
  273.1 5.6 collective-permute-done.18.refs_8_
  281.4 4.6 collective-permute-done.19.refs_7_
  288.8 3.7 collective-permute-done.20.refs_6_
  299.7 97.1 %pick.8 = (bf16[32,32,512]{2,1,0:T(8,128)(2,1)}, bf16[32,32,512]{2,1,0:T(8,128)(2,1)}, bf16[32,32,512]{2,1,0:T(8,128)(2,1)}) custom-call(s32[96]{0:T(128)} %squeeze.77.idx_ref, bf16[8,32,512]{2,1,0:T(8,128)(2,1)} %bitcast.83, bf16[8,32,512]{2,1,0:T(8,128)(2,1)} %copy-done.48, bf16[8,32,512]{2,1,0:T(8,128)(2,1)} %copy-done.54, ...), custom_call_target="tpu_custom_call" | custom-call | tf_op jit(solution)/shard_map/pick/pallas_call | solution.py:71
  399.6 17.6 %collective-permute-done.23.refs_9_ = bf16[32,32,512]{2,1,0:T(8,128)(2,1)} collective-permute-done((bf16[32,32,512]{2,1,0:T(8,128)(2,1)}, bf16[32,32,512]{2,1,0:T(8,128)(2,1)}, u32[]{:S(2)}, u32[]{:S(2)}) %collective-permute-start.23) | collective-permute-done | bytes 1048608 | tf_op jit(solution)/shard_map/ppermute | solution.py:218
  420.3 28.0 %collective-permute-done.25.refs_11_ = bf16[32,32,512]{2,1,0:T(8,128)(2,1)} collective-permute-done((bf16[32,32,512]{2,1,0:T(8,128)(2,1)}, bf16[32,32,512]{2,1,0:T(8,128)(2,1)}, u32[]{:S(2)}, u32[]{:S(2)}) %collective-permute-start.25) | collective-permute-done | bytes 1048608 | tf_op jit(solution)/shard_map/ppermute | solution.py:218
  448.3 33.7 %pick.9 = bf16[32,32,512]{2,1,0:T(8,128)(2,1)} custom-call(s32[32]{0:T(128)} %get-tuple-element.83.idx_ref, bf16[8,32,512]{2,1,0:T(8,128)(2,1)} %bitcast.84, bf16[8,32,512]{2,1,0:T(8,128)(2,1)} %copy-done.48, bf16[8,32,512]{2,1,0:T(8,128)(2,1)} %copy-done.54, bf16[8,32,512]{2,1,0:T(8,128)(2,1)} %copy-done.25, bf16[4,32,512]{2,1,0:T(8,128)(2,1)} %copy-done.62, ...), custom_call_target="tpu_custom_call" | custom-call | tf_op jit(solution)/shard_map/pick/pallas_call | solution.py:71
  497.2 6.1 message.4
  504.2 4.3 collective-permute-start.28
  509.3 4.9 collective-permute-done.27.in1
  514.2 6.7 collective-permute-done.28.in2
  531.2 6.0 collective-permute-done.33.refs_8_
  539.9 5.1 collective-permute-done.34.refs_7_
  548.0 3.9 collective-permute-done.35.refs_6_
  558.9 97.1 %pick.10 = (bf16[32,32,512]{2,1,0:T(8,128)(2,1)}, bf16[32,32,512]{2,1,0:T(8,128)(2,1)}, bf16[32,32,512]{2,1,0:T(8,128)(2,1)}) custom-call(s32[96]{0:T(128)} %squeeze.80.idx_ref, bf16[8,32,512]{2,1,0:T(8,128)(2,1)} %bitcast.78, bf16[8,32,512]{2,1,0:T(8,128)(2,1)} %copy-done.42, bf16[8,32,512]{2,1,0:T(8,128)(2,1)} %copy-done.50, ...), custom_call_target="tpu_custom_call" | custom-call | tf_op jit(solution)/shard_map/pick/pallas_call | solution.py:71
  657.6 19.3 %collective-permute-done.38.refs_9_ = bf16[32,32,512]{2,1,0:T(8,128)(2,1)} collective-permute-done((bf16[32,32,512]{2,1,0:T(8,128)(2,1)}, bf16[32,32,512]{2,1,0:T(8,128)(2,1)}, u32[]{:S(2)}, u32[]{:S(2)}) %collective-permute-start.38) | collective-permute-done | bytes 1048608 | tf_op jit(solution)/shard_map/ppermute | solution.py:218
  678.5 27.3 %collective-permute-done.40.refs_11_ = bf16[32,32,512]{2,1,0:T(8,128)(2,1)} collective-permute-done((bf16[32,32,512]{2,1,0:T(8,128)(2,1)}, bf16[32,32,512]{2,1,0:T(8,128)(2,1)}, u32[]{:S(2)}, u32[]{:S(2)}) %collective-permute-start.40) | collective-permute-done | bytes 1048608 | tf_op jit(solution)/shard_map/ppermute | solution.py:218
  705.8 33.7 %pick.11 = bf16[32,32,512]{2,1,0:T(8,128)(2,1)} custom-call(s32[32]{0:T(128)} %get-tuple-element.82.idx_ref, bf16[8,32,512]{2,1,0:T(8,128)(2,1)} %bitcast.79, bf16[8,32,512]{2,1,0:T(8,128)(2,1)} %copy-done.42, bf16[8,32,512]{2,1,0:T(8,128)(2,1)} %copy-done.50, bf16[8,32,512]{2,1,0:T(8,128)(2,1)} %copy-done.21, bf16[4,32,512]{2,1,0:T(8,128)(2,1)} %copy-done.60, ...), custom_call_target="tpu_custom_call" | custom-call | tf_op jit(solution)/shard_map/pick/pallas_call | solution.py:71
  754.6 6.1 message.5
  762.1 3.3 collective-permute-start.43
  766.3 4.7 collective-permute-done.42.in1
  771.0 6.8 collective-permute-done.43.in2
  (314 shorter events, 158.7 us)
Async XLA Ops:
  4.0 12.6 %collective-permute-start.3 = (bf16[8,32,512]{2,1,0:T(8,128)(2,1)}, bf16[8,32,512]{2,1,0:T(8,128)(2,1)S(1)}, u32[]{:S(2)}, u32[]{:S(2)}) collective-permute-start(bf16[8,32,512]{2,1,0:T(8,128)(2,1)} %bitcast.69), channel_id=1, source_target_pairs={{0,32},{4,36},{8,40},{12,44},{16,48},{20,52},{24,56},{28,60},{32,6... | collective-permute-start | bytes 786440 | tf_op jit(solution)/shard_map/ppermute | solution.py:211
  6.5 10.2 %collective-permute-start = (bf16[8,32,512]{2,1,0:T(8,128)(2,1)}, bf16[8,32,512]{2,1,0:T(8,128)(2,1)S(1)}, u32[]{:S(2)}, u32[]{:S(2)}) collective-permute-start(bf16[8,32,512]{2,1,0:T(8,128)(2,1)} %bitcast.70), channel_id=1, source_target_pairs={{0,224},{4,228},{8,232},{12,236},{16,240},{20,244},{24,248},{28,25... | collective-permute-start | bytes 786440 | tf_op jit(solution)/shard_map/ppermute | solution.py:212
  16.6 7.8 collective-permute-start.4
  16.7 7.8 collective-permute-start.1
  24.5 7.0 collective-permute-start.2
  134.8 21.9 %collective-permute-start.10 = (bf16[32,32,512]{2,1,0:T(8,128)(2,1)}, bf16[32,32,512]{2,1,0:T(8,128)(2,1)S(1)}, u32[]{:S(2)}, u32[]{:S(2)}) collective-permute-start(bf16[32,32,512]{2,1,0:T(8,128)(2,1)} %get-tuple-element.32), channel_id=1, source_target_pairs={{0,8},{4,12},{8,16},{12,20},{16,24},{20,28},{24,0},{28,4},{32,40},... | collective-permute-start | bytes 3145736 | tf_op jit(solution)/shard_map/ppermute | solution.py:218
  136.1 20.6 %collective-permute-start.8 = (bf16[32,32,512]{2,1,0:T(8,128)(2,1)}, bf16[32,32,512]{2,1,0:T(8,128)(2,1)S(1)}, u32[]{:S(2)}, u32[]{:S(2)}) collective-permute-start(bf16[32,32,512]{2,1,0:T(8,128)(2,1)} %get-tuple-element.30), channel_id=1, source_target_pairs={{0,24},{4,28},{8,0},{12,4},{16,8},{20,12},{24,16},{28,20},{32,56},... | collective-permute-start | bytes 3145736 | tf_op jit(solution)/shard_map/ppermute | solution.py:218
  137.6 42.6 %collective-permute-start.9 = (bf16[32,32,512]{2,1,0:T(8,128)(2,1)}, bf16[32,32,512]{2,1,0:T(8,128)(2,1)S(1)}, u32[]{:S(2)}, u32[]{:S(2)}) collective-permute-start(bf16[32,32,512]{2,1,0:T(8,128)(2,1)} %get-tuple-element.31), channel_id=1, source_target_pairs={{0,16},{4,20},{8,24},{12,28},{16,0},{20,4},{24,8},{28,12},{32,48},... | collective-permute-start | bytes 3145736 | tf_op jit(solution)/shard_map/ppermute | solution.py:218
  214.9 9.6 %collective-permute-start.11 = (bf16[32,32,512]{2,1,0:T(8,128)(2,1)}, bf16[32,32,512]{2,1,0:T(8,128)(2,1)S(1)}, u32[]{:S(2)}, u32[]{:S(2)}) collective-permute-start(bf16[32,32,512]{2,1,0:T(8,128)(2,1)} %pick.7), channel_id=1, source_target_pairs={{0,4},{4,0},{8,12},{12,8},{16,20},{20,16},{24,28},{28,24},{32,36},... | collective-permute-start | bytes 3145736 | tf_op jit(solution)/shard_map/ppermute | solution.py:221
  247.1 9.4 %collective-permute-start.12 = (bf16[256,512]{1,0:T(8,128)(2,1)}, bf16[256,512]{1,0:T(8,128)(2,1)S(1)}, u32[]{:S(2)}, u32[]{:S(2)}) collective-permute-start(bf16[256,512]{1,0:T(8,128)(2,1)} %get-tuple-element.34), channel_id=1, source_target_pairs={{0,1},{1,2},{2,3},{3,0},{4,5},{5,6},{6,7},{7,4},{8,9},{9,10},{10,1... | collective-permute-start | bytes 786440 | tf_op jit(solution)/shard_map/ppermute | solution.py:243
  248.4 15.0 %collective-permute-start.13 = (bf16[256,512]{1,0:T(8,128)(2,1)}, bf16[256,512]{1,0:T(8,128)(2,1)}, u32[]{:S(2)}, u32[]{:S(2)}) collective-permute-start(bf16[256,512]{1,0:T(8,128)(2,1)} %get-tuple-element.35), channel_id=1, source_target_pairs={{0,2},{1,3},{2,0},{3,1},{4,6},{5,7},{6,4},{7,5},{8,10},{9,11},{10,... | collective-permute-start | bytes 786440 | tf_op jit(solution)/shard_map/ppermute | solution.py:243
  251.0 12.4 %collective-permute-start.14 = (bf16[256,512]{1,0:T(8,128)(2,1)}, bf16[256,512]{1,0:T(8,128)(2,1)}, u32[]{:S(2)}, u32[]{:S(2)}) collective-permute-start(bf16[256,512]{1,0:T(8,128)(2,1)} %get-tuple-element.36), channel_id=1, source_target_pairs={{0,3},{1,0},{2,1},{3,2},{4,7},{5,4},{6,5},{7,6},{8,11},{9,8},{10,9... | collective-permute-start | bytes 786440 | tf_op jit(solution)/shard_map/ppermute | solution.py:243
  270.4 8.2 %collective-permute-start.18 = (bf16[8,32,512]{2,1,0:T(8,128)(2,1)S(1)}, bf16[8,32,512]{2,1,0:T(8,128)(2,1)S(1)}, u32[]{:S(2)}, u32[]{:S(2)}) collective-permute-start(bf16[8,32,512]{2,1,0:T(8,128)(2,1)S(1)} %bitcast.81), channel_id=1, source_target_pairs={{0,32},{4,36},{8,40},{12,44},{16,48},{20,52},{24,56},{28,60},{32,6... | collective-permute-start | bytes 786440 | tf_op jit(solution)/shard_map/ppermute | solution.py:211
  270.4 8.3 %collective-permute-start.15 = (bf16[8,32,512]{2,1,0:T(8,128)(2,1)S(1)}, bf16[8,32,512]{2,1,0:T(8,128)(2,1)S(1)}, u32[]{:S(2)}, u32[]{:S(2)}) collective-permute-start(bf16[8,32,512]{2,1,0:T(8,128)(2,1)S(1)} %bitcast.82), channel_id=1, source_target_pairs={{0,224},{4,228},{8,232},{12,236},{16,240},{20,244},{24,248},{28,25... | collective-permute-start | bytes 786440 | tf_op jit(solution)/shard_map/ppermute | solution.py:212
  278.7 7.3 collective-permute-start.19
  278.7 7.3 collective-permute-start.16
  396.8 20.4 %collective-permute-start.23 = (bf16[32,32,512]{2,1,0:T(8,128)(2,1)}, bf16[32,32,512]{2,1,0:T(8,128)(2,1)}, u32[]{:S(2)}, u32[]{:S(2)}) collective-permute-start(bf16[32,32,512]{2,1,0:T(8,128)(2,1)} %get-tuple-element.38), channel_id=1, source_target_pairs={{0,24},{4,28},{8,0},{12,4},{16,8},{20,12},{24,16},{28,20},{32,56},... | collective-permute-start | bytes 3145736 | tf_op jit(solution)/shard_map/ppermute | solution.py:218
  398.9 21.4 %collective-permute-start.24 = (bf16[32,32,512]{2,1,0:T(8,128)(2,1)}, bf16[32,32,512]{2,1,0:T(8,128)(2,1)}, u32[]{:S(2)}, u32[]{:S(2)}) collective-permute-start(bf16[32,32,512]{2,1,0:T(8,128)(2,1)} %get-tuple-element.39), channel_id=1, source_target_pairs={{0,16},{4,20},{8,24},{12,28},{16,0},{20,4},{24,8},{28,12},{32,48},... | collective-permute-start | bytes 3145736 | tf_op jit(solution)/shard_map/ppermute | solution.py:218
  399.4 48.9 %collective-permute-start.25 = (bf16[32,32,512]{2,1,0:T(8,128)(2,1)}, bf16[32,32,512]{2,1,0:T(8,128)(2,1)}, u32[]{:S(2)}, u32[]{:S(2)}) collective-permute-start(bf16[32,32,512]{2,1,0:T(8,128)(2,1)} %get-tuple-element.40), channel_id=1, source_target_pairs={{0,8},{4,12},{8,16},{12,20},{16,24},{20,28},{24,0},{28,4},{32,40},... | collective-permute-start | bytes 3145736 | tf_op jit(solution)/shard_map/ppermute | solution.py:218
  504.2 10.0 %collective-permute-start.27 = (bf16[256,512]{1,0:T(8,128)(2,1)}, bf16[256,512]{1,0:T(8,128)(2,1)S(1)}, u32[]{:S(2)}, u32[]{:S(2)}) collective-permute-start(bf16[256,512]{1,0:T(8,128)(2,1)} %get-tuple-element.42), channel_id=1, source_target_pairs={{0,1},{1,2},{2,3},{3,0},{4,5},{5,6},{6,7},{7,4},{8,9},{9,10},{10,1... | collective-permute-start | bytes 786440 | tf_op jit(solution)/shard_map/ppermute | solution.py:243
  504.2 16.7 %collective-permute-start.28 = (bf16[256,512]{1,0:T(8,128)(2,1)}, bf16[256,512]{1,0:T(8,128)(2,1)}, u32[]{:S(2)}, u32[]{:S(2)}) collective-permute-start(bf16[256,512]{1,0:T(8,128)(2,1)} %get-tuple-element.43), channel_id=1, source_target_pairs={{0,2},{1,3},{2,0},{3,1},{4,6},{5,7},{6,4},{7,5},{8,10},{9,11},{10,... | collective-permute-start | bytes 786440 | tf_op jit(solution)/shard_map/ppermute | solution.py:243
  508.5 12.4 %collective-permute-start.29 = (bf16[256,512]{1,0:T(8,128)(2,1)}, bf16[256,512]{1,0:T(8,128)(2,1)}, u32[]{:S(2)}, u32[]{:S(2)}) collective-permute-start(bf16[256,512]{1,0:T(8,128)(2,1)} %get-tuple-element.44), channel_id=1, source_target_pairs={{0,3},{1,0},{2,1},{3,2},{4,7},{5,4},{6,5},{7,6},{8,11},{9,8},{10,9... | collective-permute-start | bytes 786440 | tf_op jit(solution)/shard_map/ppermute | solution.py:243
  527.9 9.3 %collective-permute-start.33 = (bf16[8,32,512]{2,1,0:T(8,128)(2,1)S(1)}, bf16[8,32,512]{2,1,0:T(8,128)(2,1)S(1)}, u32[]{:S(2)}, u32[]{:S(2)}) collective-permute-start(bf16[8,32,512]{2,1,0:T(8,128)(2,1)S(1)} %bitcast.76), channel_id=1, source_target_pairs={{0,32},{4,36},{8,40},{12,44},{16,48},{20,52},{24,56},{28,60},{32,6... | collective-permute-start | bytes 786440 | tf_op jit(solution)/shard_map/ppermute | solution.py:211
  527.9 9.3 %collective-permute-start.30 = (bf16[8,32,512]{2,1,0:T(8,128)(2,1)S(1)}, bf16[8,32,512]{2,1,0:T(8,128)(2,1)S(1)}, u32[]{:S(2)}, u32[]{:S(2)}) collective-permute-start(bf16[8,32,512]{2,1,0:T(8,128)(2,1)S(1)} %bitcast.77), channel_id=1, source_target_pairs={{0,224},{4,228},{8,232},{12,236},{16,240},{20,244},{24,248},{28,25... | collective-permute-start | bytes 786440 | tf_op jit(solution)/shard_map/ppermute | solution.py:212
  537.2 7.8 collective-permute-start.34
  537.2 7.8 collective-permute-start.31
  656.0 20.8 %collective-permute-start.38 = (bf16[32,32,512]{2,1,0:T(8,128)(2,1)}, bf16[32,32,512]{2,1,0:T(8,128)(2,1)}, u32[]{:S(2)}, u32[]{:S(2)}) collective-permute-start(bf16[32,32,512]{2,1,0:T(8,128)(2,1)} %get-tuple-element.47), channel_id=1, source_target_pairs={{0,24},{4,28},{8,0},{12,4},{16,8},{20,12},{24,16},{28,20},{32,56},... | collective-permute-start | bytes 3145736 | tf_op jit(solution)/shard_map/ppermute | solution.py:218
  656.4 22.1 %collective-permute-start.39 = (bf16[32,32,512]{2,1,0:T(8,128)(2,1)}, bf16[32,32,512]{2,1,0:T(8,128)(2,1)}, u32[]{:S(2)}, u32[]{:S(2)}) collective-permute-start(bf16[32,32,512]{2,1,0:T(8,128)(2,1)} %get-tuple-element.48), channel_id=1, source_target_pairs={{0,16},{4,20},{8,24},{12,28},{16,0},{20,4},{24,8},{28,12},{32,48},... | collective-permute-start | bytes 3145736 | tf_op jit(solution)/shard_map/ppermute | solution.py:218
  656.4 49.4 %collective-permute-start.40 = (bf16[32,32,512]{2,1,0:T(8,128)(2,1)}, bf16[32,32,512]{2,1,0:T(8,128)(2,1)}, u32[]{:S(2)}, u32[]{:S(2)}) collective-permute-start(bf16[32,32,512]{2,1,0:T(8,128)(2,1)} %get-tuple-element.49), channel_id=1, source_target_pairs={{0,8},{4,12},{8,16},{12,20},{16,24},{20,28},{24,0},{28,4},{32,40},... | collective-permute-start | bytes 3145736 | tf_op jit(solution)/shard_map/ppermute | solution.py:218
  761.5 9.5 %collective-permute-start.42 = (bf16[256,512]{1,0:T(8,128)(2,1)}, bf16[256,512]{1,0:T(8,128)(2,1)S(1)}, u32[]{:S(2)}, u32[]{:S(2)}) collective-permute-start(bf16[256,512]{1,0:T(8,128)(2,1)} %get-tuple-element.51), channel_id=1, source_target_pairs={{0,1},{1,2},{2,3},{3,0},{4,5},{5,6},{6,7},{7,4},{8,9},{9,10},{10,1... | collective-permute-start | bytes 786440 | tf_op jit(solution)/shard_map/ppermute | solution.py:243
  762.1 15.7 %collective-permute-start.43 = (bf16[256,512]{1,0:T(8,128)(2,1)}, bf16[256,512]{1,0:T(8,128)(2,1)}, u32[]{:S(2)}, u32[]{:S(2)}) collective-permute-start(bf16[256,512]{1,0:T(8,128)(2,1)} %get-tuple-element.52), channel_id=1, source_target_pairs={{0,2},{1,3},{2,0},{3,1},{4,6},{5,7},{6,4},{7,5},{8,10},{9,11},{10,... | collective-permute-start | bytes 786440 | tf_op jit(solution)/shard_map/ppermute | solution.py:243
  765.5 12.4 %collective-permute-start.44 = (bf16[256,512]{1,0:T(8,128)(2,1)}, bf16[256,512]{1,0:T(8,128)(2,1)}, u32[]{:S(2)}, u32[]{:S(2)}) collective-permute-start(bf16[256,512]{1,0:T(8,128)(2,1)} %get-tuple-element.53), channel_id=1, source_target_pairs={{0,3},{1,0},{2,1},{3,2},{4,7},{5,4},{6,5},{7,6},{8,11},{9,8},{10,9... | collective-permute-start | bytes 786440 | tf_op jit(solution)/shard_map/ppermute | solution.py:243
  (106 other events, 808.2 us)
